TPU v7x, 32 devices: a whole 2x2x4 slice. The times are simulated.
32 devices in a mesh: chan: 2 (over x), row: 4 (over z), col: 4 (over y, core).
Axes of the slice: x: 2, y: 2, z: 4, core: 2. Of those that a mesh axis runs over, the one named last changes fastest.
Arguments:
- voltages: bfloat16 [2, 1024, 131072], P(None, 'chan', ('row', 'col')), may hold values from -6 to 6
- input_flags: int32 [1024], P('chan'), may hold values 0 or 1
- channel_order: int32 [128], replicated, may hold values from 0 to 127, each once
- beam_weights: bfloat16 [2, 128, 256, 1024], P(None, 'chan', 'col'), may hold values from -0.1875 to 0.1875
Outputs:
- visibility: float32 [2, 128, 1024, 1024], P(None, 'chan', 'row', 'col')
- beam_power: float32 [128, 256, 128], P('chan', 'col', 'row')
Inputs may be any that keep to these rules, and one draw needn't show every extreme that they name: `channel_order`: every fine channel appears exactly once.
All inputs are finite; a program needn't handle non-finite values. No bound on the sum of `input_flags` on one device may be relied on, other than what follows from the above.
Results may differ from a plain program's by a relative error of at most 0.005.
Values may be sent and summed in bfloat16 or wider, within the bound.
A program may use at most 448 MiB of HBM per device.

v0:
```python
import math

import jax
import jax.numpy as jnp
from jax import lax
from jax.sharding import PartitionSpec as P

NCH = 128
TAPS = 4
INTEG = 8


def passed_along(value, axis, steps):
    count = lax.axis_size(axis)
    initial, last = (max(0, -steps), min(count, count - steps))
    return lax.ppermute(value, axis, [(source, source + steps) for source in range(initial, last)])


def prototype(taps, length):
    position = jnp.arange(taps * length, dtype=jnp.float32) + 0.5
    offset = position / length - taps / 2.0
    window = 0.5 - 0.5 * jnp.cos(2.0 * math.pi * position / (taps * length))
    return (jnp.sin(math.pi * offset) / (math.pi * offset) * window).reshape(taps, length)


def dft_tables(channel_rows, length):
    sample_index = jnp.arange(length, dtype=jnp.int32)
    product = channel_rows[:, None] * sample_index[None, :] % length
    angle = 2.0 * math.pi / length * product.astype(jnp.float32)
    factor = 1.0 / math.sqrt(length)
    cosine = jnp.cos(angle) * factor
    sine = jnp.sin(angle) * factor
    real_rows = jnp.stack([cosine, sine], axis=1)
    imag_rows = jnp.stack([-sine, cosine], axis=1)
    return jnp.stack([real_rows, imag_rows], axis=1).astype(jnp.bfloat16)


def to_frames(gathered, frames, outer, inner, swapped):
    chans = gathered.shape[0]
    width = gathered.shape[1]
    split = gathered.reshape(chans, width, outer, inner, 2, frames)
    if swapped:
        order = jnp.transpose(split, (0, 4, 1, 3, 2, 5))
    else:
        order = jnp.transpose(split, (0, 4, 1, 2, 3, 5))
    return order.reshape(chans, 2, width, outer * inner * frames)


def correlate_one(left_block, right_block, frame_count):
    left_re = left_block[0]
    left_im = left_block[1]
    right_re = right_block[0]
    right_im = right_block[1]
    dims = (((1,), (1,)), ((), ()))
    vis_re = lax.dot_general(left_re, right_re, dims, preferred_element_type=jnp.float32)
    vis_re = vis_re + lax.dot_general(left_im, right_im, dims, preferred_element_type=jnp.float32)
    vis_im = lax.dot_general(left_im, right_re, dims, preferred_element_type=jnp.float32)
    vis_im = vis_im - lax.dot_general(left_re, right_im, dims, preferred_element_type=jnp.float32)
    return jnp.stack([vis_re, vis_im]) / frame_count


def correlate(left_view, right_view, frame_count):
    result = lax.map(
        lambda items: correlate_one(items[0], items[1], frame_count), (left_view, right_view)
    )
    return jnp.transpose(result, (1, 0, 2, 3))


def beams_one(weights, block):
    w_real = weights[0]
    w_imag = weights[1]
    x_real = block[0]
    x_imag = block[1]
    beam_re = jnp.dot(w_real, x_real, preferred_element_type=jnp.float32) - jnp.dot(
        w_imag, x_imag, preferred_element_type=jnp.float32
    )
    beam_im = jnp.dot(w_real, x_imag, preferred_element_type=jnp.float32) + jnp.dot(
        w_imag, x_real, preferred_element_type=jnp.float32
    )
    return jnp.stack([beam_re, beam_im], axis=1)


def form_beams(weights, view):
    by_channel = jnp.transpose(weights, (1, 0, 2, 3))
    return lax.map(lambda items: beams_one(items[0], items[1]), (by_channel, view))


def integrate(voltage):
    power = voltage[:, :, 0] * voltage[:, :, 0] + voltage[:, :, 1] * voltage[:, :, 1]
    return power.reshape(power.shape[0], power.shape[1], -1, INTEG).mean(axis=-1)


def on_device(voltages, input_flags, channel_order, beam_weights):
    masked = voltages * input_flags.astype(jnp.bfloat16)[None, :, None]
    local_inputs = masked.shape[1]
    frames = masked.shape[2] // NCH
    history = passed_along(masked[:, :, masked.shape[2] - (TAPS - 1) * NCH :], ("row", "col"), 1)
    joined = jnp.concatenate([history, masked], axis=2)
    blocks = joined.reshape(2, local_inputs, frames + TAPS - 1, NCH)
    coeffs = prototype(TAPS, NCH)
    filtered = jnp.zeros((2, local_inputs, frames, NCH), jnp.float32)
    for tap_index in range(TAPS):
        filtered = filtered + coeffs[tap_index] * blocks[
            :, :, tap_index : tap_index + frames
        ].astype(jnp.float32)
    filtered = filtered.astype(jnp.bfloat16)
    tables = dft_tables(channel_order, NCH)
    spectrum = jnp.einsum(
        "kqpn,pifn->kiqf",
        tables.astype(jnp.float32),
        filtered.astype(jnp.float32),
        precision=lax.Precision.HIGHEST,
    ).astype(jnp.bfloat16)
    spectrum = spectrum.reshape(NCH, local_inputs, 2 * frames)
    turned = lax.all_to_all(spectrum, "chan", split_axis=0, concat_axis=1, tiled=True)
    row_count = lax.axis_size("row")
    col_count = lax.axis_size("col")
    total_frames = frames * row_count * col_count
    row_turned = lax.all_to_all(turned, "row", split_axis=1, concat_axis=2, tiled=True)
    row_all = lax.all_gather(row_turned, "col", axis=2, tiled=True)
    col_turned = lax.all_to_all(turned, "col", split_axis=1, concat_axis=2, tiled=True)
    col_all = lax.all_gather(col_turned, "row", axis=2, tiled=True)
    row_view = to_frames(row_all, frames, col_count, row_count, True)
    col_view = to_frames(col_all, frames, row_count, col_count, False)
    visibility = correlate(row_view, col_view, total_frames)
    weights_all = lax.all_gather(beam_weights, "col", axis=2, tiled=True)
    local_view = to_frames(turned, frames, 1, 1, False)
    voltage = form_beams(weights_all, local_view)
    own_power = integrate(voltage)
    beam_power = lax.all_to_all(own_power, "col", split_axis=1, concat_axis=2, tiled=True)
    return (visibility, beam_power)


def solution(mesh):
    placed = (P(None, "chan", ("row", "col")), P("chan"), P(), P(None, "chan", "col", None))
    return jax.shard_map(
        on_device,
        mesh=mesh,
        in_specs=placed,
        out_specs=(P(None, "chan", "row", "col"), P("chan", "col", "row")),
        check_vma=False,
    )
```

profile of v0, /device:TPU:13, one launch (start us, length us, event | category | flops | bytes accessed | tf_op | source)
XLA Modules:
  0.0 2969.4 jit_solution(14920346079124077078)
XLA Ops:
  7.2 14.1 copy.92
  21.3 23.0 copy.77
  44.3 11.6 broadcast_multiply_fusion
  56.0 3.7 collective-permute-start
  60.2 8.5 collective-permute-done
  68.7 8.3 pad_maximum_fusion
  77.0 30.7 %fusion.20 = bf16[128,512,2,64]{0,1,2,3:T(8,128)(2,1)} fusion(bf16[128,1,2,128]{3,0,2,1:T(8,128)(2,1)S(1)} %get-tuple-element.105, bf16[128,1,2,128]{3,0,2,1:T(8,128)(2,1)S(1)} %get-tuple-element.104, bf16[2,512,67,128]{1,3,2,0:T(8,128)(2,1)} %bitcast.174, f32[128]{0:T(128)S(1)} %get-tuple-element.107, f32[128]{0:T(128)S(1)} %get-tuple-element.108, ...), kind=kOutput, calls=%fused_computation.37 | convolution fusion | flops 4404281344 | bytes 84019200 | tf_op jit(solution)/shard_map/kqpn,pifn->kiqf/dot_general | solution.py:108
  107.7 23.3 copy.79
  131.0 181.9 %all_to_all.72 = bf16[128,512,128]{1,2,0:T(8,128)(2,1)} all-to-all(bf16[128,512,128]{1,2,0:T(8,128)(2,1)} %bitcast.170), channel_id=1, replica_groups=mesh['chan'=2,'row'=4,'col'=4] {'chan'}, dimensions={0} | all-to-all | bytes 33554432 | tf_op jit(solution)/shard_map/all_to_all | solution.py:115
  313.0 22.8 copy.102
  335.7 262.5 %all_to_all.73 = bf16[64,1024,128]{2,0,1:T(8,128)(2,1)} all-to-all(bf16[64,1024,128]{2,0,1:T(8,128)(2,1)} %bitcast.166), channel_id=1, replica_groups=mesh['chan'=2,'row'=4,'col'=4] {'col'}, dimensions={1} | all-to-all | bytes 33554432 | tf_op jit(solution)/shard_map/all_to_all | solution.py:121
  598.2 24.8 copy.87
  623.1 814.1 %all_to_all.74 = bf16[64,1024,128]{2,0,1:T(8,128)(2,1)} all-to-all(bf16[64,1024,128]{2,0,1:T(8,128)(2,1)} %bitcast.167), channel_id=1, replica_groups=mesh['chan'=2,'row'=4,'col'=4] {'row'}, dimensions={1} | all-to-all | bytes 33554432 | tf_op jit(solution)/shard_map/all_to_all | solution.py:119
  1437.2 24.8 copy.83
  1462.0 30.9 %copy.93 = bf16[64,2,512,128]{2,1,3,0:T(2,128)(2,1)} copy(bf16[64,2,512,128]{2,3,0,1:T(8,128)(2,1)} %bitcast.165) | data formatting | bytes 33554432 | tf_op jit(solution)/shard_map/all_to_all | solution.py:115
  1493.0 27.5 reshape.221
  1520.5 388.6 %while.21 = (s32[]{:T(128)}, f32[64,256,2,64]{1,3,2,0:T(8,128)}, bf16[64,2,256,1024]{3,2,1,0:T(8,128)(2,1)}, bf16[64,2,1024,64]{2,3,1,0:T(8,128)(2,1)}, s32[]{:T(128)}, /*index=5*/s32[]{:T(128)}, s32[]{}) while((s32[]{:T(128)}, f32[64,256,2,64]{1,3,2,0:T(8,128)}, bf16[64,2,256,1024]{3,2,1,0:T(8,128)(2,1)}, ...), condition=%wide.region_3.4_spmd, body=%wide.region_2.3_spmd.sunk | while | flops 134283264 | bytes 3282529 | solution.py:85
  1909.0 5.4 bitcast_reduce_fusion
  1916.4 7.0 all-to-all-start.3
  1923.5 7.1 all-to-all-done.3
  1931.0 2.1 reduce
  1936.0 137.6 %all-gather.6.cloned.1.call-done = bf16[64,256,2048]{1,2,0:T(8,128)(2,1)} async-done(((bf16[64,256,512]{1,2,0:T(8,128)(2,1)}), bf16[64,256,2048]{1,2,0:T(8,128)(2,1)}) %all-gather.6.cloned.1.call-update) | async-done | bytes 67108880 | tf_op jit(solution)/shard_map/all_gather | solution.py:122
  2073.5 54.9 %copy.88 = bf16[64,2,256,4,4,64]{2,5,4,3,1,0:T(8,128)(2,1)} copy(bf16[64,2,256,4,4,64]{2,5,1,4,3,0:T(8,128)(2,1)} %bitcast.40) | data formatting | bytes 134217728 | tf_op jit(solution)/shard_map/transpose | solution.py:45
  2128.5 341.1 %all-gather.4.cloned.1.call-done = bf16[64,256,2048]{1,2,0:T(8,128)(2,1)} async-done(((bf16[64,256,512]{1,2,0:T(8,128)(2,1)}), bf16[64,256,2048]{1,2,0:T(8,128)(2,1)}) %all-gather.4.cloned.1.call-update) | async-done | bytes 67108880 | tf_op jit(solution)/shard_map/all_gather | solution.py:120
  2469.5 44.1 %copy.84 = bf16[64,2,256,4,4,64]{2,5,4,3,1,0:T(8,128)(2,1)} copy(bf16[64,2,256,4,4,64]{2,5,1,3,4,0:T(8,128)(2,1)} %bitcast.31) | data formatting | bytes 134217728 | tf_op jit(solution)/shard_map/transpose | solution.py:43
  2513.6 449.3 %while.20 = (s32[]{:T(128)}, f32[64,2,256,256]{3,2,0,1:T(8,128)}, bf16[64,2,256,1024]{2,3,1,0:T(8,128)(2,1)}, bf16[64,2,256,1024]{2,3,1,0:T(8,128)(2,1)}, s32[]{:T(128)}, /*index=5*/s32[]{:T(128)}, s32[]{}) while((s32[]{:T(128)}, f32[64,2,256,256]{3,2,0,1:T(8,128)}, bf16[64,2,256,1024]{2,3,1,0:T(8,128)(2,1)}, ...), condition=%wide.region_1.2_spmd, body=%wide.region_0.1_spmd.sunk | while | flops 537264128 | bytes 6821473 | solution.py:63
  2515.1 1.5 fusion.50
  2529.1 1.5 fusion.50
  2550.2 1.5 fusion.50
  2571.3 1.5 fusion.50
  2592.3 1.5 fusion.50
  2613.4 1.5 fusion.50
  2634.4 1.5 fusion.50
  2655.5 1.5 fusion.50
  2676.6 1.5 fusion.50
  2697.6 1.5 fusion.50
  2718.7 1.5 fusion.50
  2739.7 1.5 fusion.50
  2760.8 1.5 fusion.50
  2781.9 1.5 fusion.50
  2802.9 1.5 fusion.50
  2824.0 1.5 fusion.50
  2845.0 1.5 fusion.50
  2866.1 1.5 fusion.50
  2887.2 1.5 fusion.50
  2908.2 1.5 fusion.50
  2929.3 1.5 fusion.50
  2950.4 1.5 fusion.50
  (644 shorter events, 807.6 us)
Async XLA Ops:
  7.2 1513.3 %all-gather.8.cloned.1.call-start = ((), (), s32[]{:S(2)}) async-start(), calls=%async_computation.6 | async-start | bytes 83886080 | tf_op jit(solution)/shard_map/all_gather | solution.py:126
  21.3 23.0 copy-start
  21.3 2052.2 %all-gather.6.cloned.1.call-start = ((), (), s32[]{:S(2)}) async-start(), calls=%async_computation.5 | async-start | bytes 83886080 | tf_op jit(solution)/shard_map/all_gather | solution.py:122
  44.3 15.5 copy-start.1
  56.0 12.7 collective-permute-start
  623.0 1846.5 %all-gather.4.cloned.1.call-start = ((), (), s32[]{:S(2)}) async-start(), calls=%async_computation.4 | async-start | bytes 83886080 | tf_op jit(solution)/shard_map/all_gather | solution.py:120
  1916.4 14.1 all-to-all-start.3
Sparse Core Ops, SparseCore 0:
  21.4 456.6 all-gather.7
  623.2 1450.3 all-gather.5
  2075.1 394.3 all-gather.3
where the time goes:
time: 2990 us; the launch traced here: 2970 us
  blocking collectives  1260 us (42%)
  matrix products  771 us (26%)
  waiting for transfers between devices  494 us (17%)
  local copies, waits for them, and re-layouts  295 us (10%)
  other arithmetic  124 us (4%)
    all_to_all x1, blocking collectives, on_device(): lax.all_to_all(turned, 'row', split_axis=1, concat_axis=2, tiled=True)  814 us
    all_gather x1, waiting for transfers between devices, on_device(): row_all = lax.all_gather(row_turned, 'col', axis=2, tiled=True)  341 us
    all_to_all x1, blocking collectives, on_device(): lax.all_to_all(turned, 'col', split_axis=1, concat_axis=2, tiled=True)  262 us
    all_to_all x1, blocking collectives, on_device(): lax.all_to_all(spectrum, 'chan', split_axis=0, concat_axis=1, tiled=True)  182 us
    all_gather x1, waiting for transfers between devices, on_device(): col_all = lax.all_gather(col_turned, 'row', axis=2, tiled=True)  138 us
    dot_general x64, matrix products, correlate_one(): lax.dot_general(left_re, right_im, dims, preferred_element_type=jnp.float32)  98.7 us
    dot_general x64, matrix products, correlate_one(): lax.dot_general(left_im, right_im, dims, preferred_element_type=jnp.float32)  98.6 us
    dot_general x64, matrix products, correlate_one(): lax.dot_general(left_re, right_re, dims, preferred_element_type=jnp.float32)  98.5 us
  transfers between devices with their start and end apart: 5, of which 4 were waited for; matrix products, arithmetic and copies ran while one was open for 23% of the time, Pallas kernels for 0%

commit v1 on v0

--- a/solution.py
+++ b/solution.py
@@ -1,8 +1,11 @@
+import functools
 import math
 
 import jax
 import jax.numpy as jnp
 from jax import lax
+from jax.experimental import pallas as pl
+from jax.experimental.pallas import tpu as pltpu
 from jax.sharding import PartitionSpec as P
 
 NCH = 128
@@ -90,7 +93,7 @@
     return power.reshape(power.shape[0], power.shape[1], -1, INTEG).mean(axis=-1)
 
 
-def on_device(voltages, input_flags, channel_order, beam_weights):
+def channelize(voltages, input_flags, channel_order):
     masked = voltages * input_flags.astype(jnp.bfloat16)[None, :, None]
     local_inputs = masked.shape[1]
     frames = masked.shape[2] // NCH
@@ -112,6 +115,12 @@
         precision=lax.Precision.HIGHEST,
     ).astype(jnp.bfloat16)
     spectrum = spectrum.reshape(NCH, local_inputs, 2 * frames)
+    return spectrum
+
+
+def by_panels(voltages, input_flags, channel_order, beam_weights):
+    spectrum = channelize(voltages, input_flags, channel_order)
+    frames = spectrum.shape[2] // 2
     turned = lax.all_to_all(spectrum, "chan", split_axis=0, concat_axis=1, tiled=True)
     row_count = lax.axis_size("row")
     col_count = lax.axis_size("col")
@@ -131,6 +140,309 @@
     return (visibility, beam_power)
 
 
+MESH = pl.DeviceIdType.MESH
+
+
+def sizes():
+    return lax.axis_size("chan"), lax.axis_size("row"), lax.axis_size("col")
+
+
+def turn_kernel(cs, rs, qs, spec_ref, weight_ref, x_ref, w_ref, send, recv, wsend, wrecv, local):
+    c, r, q = (lax.axis_index(name) for name in ("chan", "row", "col"))
+    cells = rs * qs
+    devices = cs * cells
+    me = r * qs + q
+    here = c * cells + me
+    own = spec_ref.shape[0] // devices
+    inputs = spec_ref.shape[1]
+    lanes = spec_ref.shape[2]
+    beams = weight_ref.shape[2]
+
+    def place(chan, cell):
+        return x_ref.at[
+            :,
+            pl.ds(pl.multiple_of(chan * inputs, inputs), inputs),
+            pl.ds(pl.multiple_of(cell * lanes, lanes), lanes),
+        ]
+
+    def spectra(step, outgoing):
+        if outgoing:
+            chan, cell = (c + step % cs) % cs, (me + step // cs) % cells
+            target = place(c, me)
+            slot = here
+        else:
+            chan, cell = (c + cs - step % cs) % cs, (me + cells - step // cs) % cells
+            target = place(chan, cell)
+            slot = chan * cells + cell
+        return pltpu.make_async_remote_copy(
+            src_ref=spec_ref.at[pl.ds((chan * cells + cell) * own, own)],
+            dst_ref=target,
+            send_sem=send.at[chan * cells + cell],
+            recv_sem=recv.at[slot],
+            device_id=(chan, cell // qs, cell % qs),
+            device_id_type=MESH,
+        )
+
+    def weights(step, outgoing):
+        if outgoing:
+            peer = (q + step) % qs
+            slot = q
+        else:
+            peer = (q + qs - step) % qs
+            slot = peer
+        return pltpu.make_async_remote_copy(
+            src_ref=weight_ref.at[:, pl.ds((r * qs + peer) * own, own)],
+            dst_ref=w_ref.at[:, :, pl.ds(pl.multiple_of(slot * beams, beams), beams)],
+            send_sem=wsend.at[peer],
+            recv_sem=wrecv.at[slot],
+            device_id=(c, r, peer),
+            device_id_type=MESH,
+        )
+
+    def start(step, carry):
+        spectra(step, True).start()
+        return carry
+
+    def start_weights(step, carry):
+        weights(step, True).start()
+        return carry
+
+    lax.fori_loop(1, devices, start, 0)
+    lax.fori_loop(1, qs, start_weights, 0)
+    stay = pltpu.make_async_copy(spec_ref.at[pl.ds(here * own, own)], place(c, me), local.at[0])
+    keep = pltpu.make_async_copy(
+        weight_ref.at[:, pl.ds(me * own, own)],
+        w_ref.at[:, :, pl.ds(pl.multiple_of(q * beams, beams), beams)],
+        local.at[1],
+    )
+    stay.start()
+    keep.start()
+
+    def finish(step, carry):
+        spectra(step, True).wait_send()
+        spectra(step, False).wait_recv()
+        return carry
+
+    def finish_weights(step, carry):
+        weights(step, True).wait_send()
+        weights(step, False).wait_recv()
+        return carry
+
+    lax.fori_loop(1, devices, finish, 0)
+    lax.fori_loop(1, qs, finish_weights, 0)
+    stay.wait()
+    keep.wait()
+
+
+def turn(spectrum, beam_weights):
+    cs, rs, qs = sizes()
+    devices = cs * rs * qs
+    own = spectrum.shape[0] // devices
+    anywhere = pl.BlockSpec(memory_space=pl.ANY)
+    return pl.pallas_call(
+        functools.partial(turn_kernel, cs, rs, qs),
+        out_shape=(
+            jax.ShapeDtypeStruct(
+                (own, spectrum.shape[1] * cs, spectrum.shape[2] * rs * qs), spectrum.dtype
+            ),
+            jax.ShapeDtypeStruct(
+                (2, own, beam_weights.shape[2] * qs, beam_weights.shape[3]), beam_weights.dtype
+            ),
+        ),
+        in_specs=[anywhere] * 2,
+        out_specs=(anywhere,) * 2,
+        scratch_shapes=[
+            pltpu.SemaphoreType.DMA((devices,)),
+            pltpu.SemaphoreType.DMA((devices,)),
+            pltpu.SemaphoreType.DMA((qs,)),
+            pltpu.SemaphoreType.DMA((qs,)),
+            pltpu.SemaphoreType.DMA((2,)),
+        ],
+        compiler_params=pltpu.CompilerParams(has_side_effects=True),
+        name="turn",
+    )(spectrum, beam_weights)
+
+
+def deliver_kernel(rs, qs, vis_ref, power_ref, block_ref, part_ref, send, recv, psend, precv, local):
+    c, r, q = (lax.axis_index(name) for name in ("chan", "row", "col"))
+    cells = rs * qs
+    me = r * qs + q
+    own, height, width = vis_ref.shape[1], block_ref.shape[2], block_ref.shape[3]
+
+    def piece(row, col):
+        return vis_ref.at[
+            :,
+            :,
+            pl.ds(pl.multiple_of(row * height, height), height),
+            pl.ds(pl.multiple_of(col * width, width), width),
+        ]
+
+    def copies(step, outgoing):
+        if outgoing:
+            cell = (me + step) % cells
+            slot = me
+        else:
+            cell = (me + cells - step) % cells
+            slot = cell
+        device = (c, cell // qs, cell % qs)
+        block = pltpu.make_async_remote_copy(
+            src_ref=piece(cell // qs, cell % qs),
+            dst_ref=block_ref.at[:, pl.ds(slot * own, own)],
+            send_sem=send.at[cell],
+            recv_sem=recv.at[slot],
+            device_id=device,
+            device_id_type=MESH,
+        )
+        part = pltpu.make_async_remote_copy(
+            src_ref=power_ref.at[cell],
+            dst_ref=part_ref.at[slot],
+            send_sem=psend.at[cell],
+            recv_sem=precv.at[slot],
+            device_id=device,
+            device_id_type=MESH,
+        )
+        return block, part
+
+    def start(step, carry):
+        for copy in copies(step, True):
+            copy.start()
+        return carry
+
+    lax.fori_loop(1, cells, start, 0)
+    stay = pltpu.make_async_copy(piece(r, q), block_ref.at[:, pl.ds(me * own, own)], local.at[0])
+    keep = pltpu.make_async_copy(power_ref.at[me], part_ref.at[me], local.at[1])
+    stay.start()
+    keep.start()
+
+    def finish(step, carry):
+        for copy in copies(step, True):
+            copy.wait_send()
+        for copy in copies(step, False):
+            copy.wait_recv()
+        return carry
+
+    lax.fori_loop(1, cells, finish, 0)
+    stay.wait()
+    keep.wait()
+
+
+def deliver(visibility, power):
+    _, rs, qs = sizes()
+    cells = rs * qs
+    own = visibility.shape[1]
+    anywhere = pl.BlockSpec(memory_space=pl.ANY)
+    return pl.pallas_call(
+        functools.partial(deliver_kernel, rs, qs),
+        out_shape=(
+            jax.ShapeDtypeStruct(
+                (2, own * cells, visibility.shape[2] // rs, visibility.shape[3] // qs),
+                visibility.dtype,
+            ),
+            jax.ShapeDtypeStruct(power.shape, power.dtype),
+        ),
+        in_specs=[anywhere] * 2,
+        out_specs=(anywhere,) * 2,
+        scratch_shapes=[pltpu.SemaphoreType.DMA((cells,))] * 4 + [pltpu.SemaphoreType.DMA((2,))],
+        compiler_params=pltpu.CompilerParams(has_side_effects=True),
+        name="deliver",
+    )(visibility, power)
+
+
+def products_kernel(frame_count, tile, x_ref, w_ref, swap_ref, pool_ref, vis_ref, power_ref, y_ref):
+    inputs, depth = x_ref.shape[1], x_ref.shape[2]
+    lanes = swap_ref.shape[0]
+    across = (((1,), (1,)), ((), ()))
+    for start in range(0, depth, lanes):
+        y_ref[:, start : start + lanes] = jnp.dot(
+            x_ref[0, :, start : start + lanes], swap_ref[...], preferred_element_type=jnp.float32
+        ).astype(jnp.bfloat16)
+
+    def rows(step, carry):
+        at = pl.ds(pl.multiple_of(step * tile, tile), tile)
+        re = lax.dot_general(x_ref[0, at, :], x_ref[0], across, preferred_element_type=jnp.float32)
+        vis_ref[0, 0, at, :] = (re / frame_count).astype(vis_ref.dtype)
+        im = lax.dot_general(y_ref[at, :], x_ref[0], across, preferred_element_type=jnp.float32)
+        vis_ref[1, 0, at, :] = (im / frame_count).astype(vis_ref.dtype)
+        return carry
+
+    lax.fori_loop(0, inputs // tile, rows, 0)
+    power_ref[...] = jnp.zeros_like(power_ref)
+    width = 4 * lanes if depth % (4 * lanes) == 0 else lanes
+
+    def columns(step, carry):
+        at = pl.ds(pl.multiple_of(step * width, width), width)
+        beam = jnp.dot(w_ref[0, 0], x_ref[0, :, at], preferred_element_type=jnp.float32)
+        beam = beam - jnp.dot(w_ref[1, 0], y_ref[:, at], preferred_element_type=jnp.float32)
+        square = beam * beam
+        high = square.astype(jnp.bfloat16)
+        low = (square - high.astype(jnp.float32)).astype(jnp.bfloat16)
+        pool = pool_ref[at, :]
+        power_ref[0] += jnp.dot(high, pool, preferred_element_type=jnp.float32) + jnp.dot(
+            low, pool, preferred_element_type=jnp.float32
+        )
+        return carry
+
+    lax.fori_loop(0, depth // width, columns, 0)
+
+
+def products(x, weights, frames):
+    own, inputs, depth = x.shape
+    beams = weights.shape[2]
+    bins = depth // (2 * INTEG)
+    lanes = 2 * frames
+    source = jnp.arange(lanes)[:, None]
+    goal = jnp.arange(lanes)[None, :]
+    swap = jnp.where(source == goal + frames, 1.0, 0.0) - jnp.where(source + frames == goal, 1.0, 0.0)
+    at = jnp.arange(depth)
+    frame = at // lanes * frames + at % frames
+    pool = jnp.where(frame[:, None] // INTEG == jnp.arange(bins)[None, :], 1.0 / INTEG, 0.0)
+    return pl.pallas_call(
+        functools.partial(products_kernel, depth // 2, min(inputs, 256)),
+        grid=(own,),
+        out_shape=(
+            jax.ShapeDtypeStruct((2, own, inputs, inputs), jnp.bfloat16),
+            jax.ShapeDtypeStruct((own, beams, bins), jnp.float32),
+        ),
+        in_specs=[
+            pl.BlockSpec((1, inputs, depth), lambda j: (j, 0, 0)),
+            pl.BlockSpec((2, 1, beams, inputs), lambda j: (0, j, 0, 0)),
+            pl.BlockSpec((lanes, lanes), lambda j: (0, 0)),
+            pl.BlockSpec((depth, bins), lambda j: (0, 0)),
+        ],
+        out_specs=(
+            pl.BlockSpec((2, 1, inputs, inputs), lambda j: (0, j, 0, 0)),
+            pl.BlockSpec((1, beams, bins), lambda j: (j, 0, 0)),
+        ),
+        scratch_shapes=[pltpu.VMEM((inputs, depth), jnp.bfloat16)],
+        compiler_params=pltpu.CompilerParams(vmem_limit_bytes=60 << 20),
+        name="products",
+    )(x, weights, swap.astype(jnp.bfloat16), pool.astype(jnp.bfloat16))
+
+
+def by_channels(voltages, input_flags, channel_order, beam_weights):
+    _, rs, qs = sizes()
+    spectrum = channelize(voltages, input_flags, channel_order)
+    frames = spectrum.shape[2] // 2
+    x, weights = turn(spectrum, beam_weights)
+    visibility, power = products(x, weights, frames)
+    own, beams, bins = power.shape
+    split = power.reshape(own, qs, beams // qs, rs, bins // rs)
+    parts = jnp.transpose(split, (3, 1, 0, 2, 4)).reshape(rs * qs, -1, 2 * frames)
+    block, part = deliver(visibility, parts)
+    beam_power = part.reshape(rs * qs * own, beams // qs, bins // rs)
+    return (block.astype(jnp.float32), beam_power)
+
+
+def on_device(voltages, input_flags, channel_order, beam_weights):
+    cs, rs, qs = sizes()
+    lanes = 2 * (voltages.shape[2] // NCH)
+    if NCH % (cs * rs * qs) == 0 and lanes % 128 == 0:
+        plan = by_channels
+    else:
+        plan = by_panels
+    return plan(voltages, input_flags, channel_order, beam_weights)
+
+
 def solution(mesh):
     placed = (P(None, "chan", ("row", "col")), P("chan"), P(), P(None, "chan", "col", None))
     return jax.shard_map(

time: 2990 us -> 983 us (0.33)
  blocking collectives: 1260 us -> 0 us
  Pallas kernels: 0 us -> 828 us
  matrix products: 771 us -> 30.7 us
  waiting for transfers between devices: 494 us -> 6.6 us
  local copies, waits for them, and re-layouts: 295 us -> 72.5 us
  other arithmetic: 124 us -> 38 us
    all_to_all x3 -> x0, blocking collectives: 1260 us -> none  [the longest x1 814 us: on_device(): lax.all_to_all(turned, 'row', split_axis=1, concat_axis=2, tiled=True)]
    pallas_call x0 -> x3, Pallas kernels: none -> 828 us  [the longest x1 387 us: turn(): pl.pallas_call(functools.partial(turn_kernel, cs, rs, qs), out_shape=(jax...]
    dot_general x513 -> x1, matrix products: 771 us -> 30.7 us  [channelize(): jnp.einsum('kqpn,pifn->kiqf', tables.astype(jnp.float32), filtered.astype...]
    all_gather x3 -> x0, waiting for transfers between devices: 479 us -> none  [the longest x1 341 us: on_device(): row_all = lax.all_gather(row_turned, 'col', axis=2, tiled=True)]
    all_to_all x7 -> x0, local copies, waits for them, and re-layouts: 106 us -> none  [the longest x2 53.7 us: on_device(): lax.all_to_all(spectrum, 'chan', split_axis=0, concat_axis=1, tiled=True)]
    transpose x2 -> x1, local copies, waits for them, and re-layouts: 99 us -> 0.83 us  [by_channels(): jnp.transpose(split, (3, 1, 0, 2, 4)).reshape(rs * qs, -1, 2 * frames)]
    dynamic_update_slice x128 -> x0, other arithmetic: 95.9 us -> none  [the longest x64 53.5 us: correlate(): lax.map(lambda items: correlate_one(items[0], items[1], frame_count), (le...]
  transfers between devices with their start and end apart: 5 -> 1, of which waited for: 4 -> 1; matrix products, arithmetic and copies ran while one was open for 23% -> 0% of each run, Pallas kernels for 0% -> 0%
where the time goes in v1:
time: 983 us; the launch traced here: 981 us
  Pallas kernels  828 us (84%)
  local copies, waits for them, and re-layouts  72.5 us (7%)
  other arithmetic  38 us (4%)
  matrix products  30.7 us (3%)
    pallas_call x1, Pallas kernels, turn(): pl.pallas_call(functools.partial(turn_kernel, cs, rs, qs), out_shape=(jax...  387 us
    pallas_call x1, Pallas kernels, deliver(): pl.pallas_call(functools.partial(deliver_kernel, rs, qs), out_shape=(jax....  378 us
    pallas_call x1, Pallas kernels, products(): pl.pallas_call(functools.partial(products_kernel, depth // 2, min(inputs,...  62.6 us
    dot_general x1, matrix products, channelize(): jnp.einsum('kqpn,pifn->kiqf', tables.astype(jnp.float32), filtered.astype...  30.7 us
    convert_element_type x1, local copies, waits for them, and re-layouts, channelize(): spectrum = jnp.einsum('kqpn,pifn->kiqf', tables.astype(jnp.float32), filt...  23.3 us
    unnamed x8, local copies, waits for them, and re-layouts  22.8 us
    reshape x1, local copies, waits for them, and re-layouts, channelize(): spectrum = spectrum.reshape(NCH, local_inputs, 2 * frames)  22.1 us
  transfers between devices with their start and end apart: 1, of which 1 were waited for; matrix products, arithmetic and copies ran while one was open for 0% of the time, Pallas kernels for 0%

profile of v1, /device:TPU:13, one launch (start us, length us, event | category | flops | bytes accessed | tf_op | source)
XLA Modules:
  0.0 980.6 jit_solution(6653444241687415204)
XLA Ops:
  0.6 0.0 copy-start.1
  0.6 21.2 %copy.13 = bf16[2,512,8192]{1,2,0:T(8,128)(2,1)} copy(bf16[2,512,8192]{2,1,0:T(8,128)(2,1)} %param.4) | data formatting | bytes 33554432 | tf_op args[0]
  21.9 0.0 copy-done.1
  21.9 0.0 copy-start.2
  21.9 8.7 broadcast_multiply_fusion
  30.6 0.1 slice.40
  30.7 3.7 collective-permute-start
  34.4 0.1 fusion.27
  34.5 0.0 copy-done.2
  34.5 0.3 fusion.14
  34.9 0.7 subtract_convert_fusion.swap_ref
  35.6 1.1 select_convert_fusion.pool_ref
  36.7 6.6 collective-permute-done
  43.3 8.3 pad_maximum_fusion
  51.6 30.7 %fusion.1 = bf16[128,512,2,64]{0,1,2,3:T(8,128)(2,1)} fusion(bf16[128,1,2,128]{3,0,2,1:T(8,128)(2,1)S(1)} %get-tuple-element.19, bf16[128,1,2,128]{3,0,2,1:T(8,128)(2,1)S(1)} %get-tuple-element.18, bf16[2,512,67,128]{1,3,2,0:T(8,128)(2,1)} %bitcast.26, f32[128]{0:T(128)S(1)} %get-tuple-element.21, f32[128]{0:T(128)S(1)} %get-tuple-element.22, ...), kind=kOutput, calls=%fused_computation.4 | convolution fusion | flops 4404281344 | bytes 84019200 | tf_op jit(solution)/shard_map/kqpn,pifn->kiqf/dot_general | solution.py:111
  82.3 23.3 %copy.15 = bf16[128,512,2,64]{1,3,2,0:T(8,128)(2,1)} copy(bf16[128,512,2,64]{0,1,2,3:T(8,128)(2,1)} %fusion.1) | data formatting | bytes 33554432 | tf_op jit(solution)/shard_map/convert_element_type | solution.py:116
  105.7 22.1 %copy.16.spec_ref = bf16[128,512,128]{2,1,0:T(8,128)(2,1)} copy(bf16[128,512,128]{1,2,0:T(8,128)(2,1)} %bitcast.25) | data formatting | bytes 33554432 | tf_op jit(solution)/shard_map/reshape | solution.py:117
  127.7 387.4 %turn.1 = (bf16[4,1024,2048]{2,1,0:T(8,128)(2,1)}, bf16[2,4,256,1024]{3,2,1,0:T(8,128)(2,1)}) custom-call(bf16[128,512,128]{2,1,0:T(8,128)(2,1)} %copy.16.spec_ref, bf16[2,64,64,1024]{3,2,1,0:T(8,128)(2,1)} %weight_ref.1), custom_call_target="tpu_custom_call" | custom-call | tf_op jit(solution)/shard_map/turn/pallas_call | solution.py:242
  515.1 62.6 %products.1 = (bf16[2,4,1024,1024]{3,2,1,0:T(8,128)(2,1)}, f32[4,256,128]{2,1,0:T(8,128)}) custom-call(bf16[4,1024,2048]{2,1,0:T(8,128)(2,1)} %get-tuple-element.8.x_ref, bf16[2,4,256,1024]{3,2,1,0:T(8,128)(2,1)} %get-tuple-element.9.w_ref, bf16[128,128]{1,0:T(8,128)(2,1)} %subtract_convert_fusion.swap_ref, bf16[2048,128]{1,0:T(8,128)(2,1)} %select_convert_fusion.pool_ref), custom_call_target="tpu_custom_call" | custom-call | tf_op jit(solution)/shard_map/products/pallas_call | solution.py:399
  577.7 1.2 copy.17
  579.0 0.5 reshape.219
  579.4 0.8 copy.18
  580.3 1.3 reshape.220.power_ref
  581.6 378.3 %deliver.1 = (bf16[2,64,256,256]{3,2,1,0:T(8,128)(2,1)}, f32[16,64,128]{2,1,0:T(8,128)}) custom-call(bf16[2,4,1024,1024]{3,2,1,0:T(8,128)(2,1)} %get-tuple-element.10.vis_ref, f32[16,64,128]{2,1,0:T(8,128)} %reshape.220.power_ref), custom_call_target="tpu_custom_call" | custom-call | tf_op jit(solution)/shard_map/deliver/pallas_call | solution.py:334
  959.8 0.0 copy-start
  959.8 18.7 %convert_element_type.65 = f32[2,64,256,256]{3,2,1,0:T(8,128)} convert(bf16[2,64,256,256]{3,2,1,0:T(8,128)(2,1)} %get-tuple-element.12) | non-fusion elementwise | flops 8388608 | bytes 50331648 | tf_op jit(solution)/shard_map/convert_element_type | solution.py:433
  978.5 0.0 copy-done
  978.5 0.5 reshape.221
  979.0 1.6 copy.19
  (5 shorter events, 0.0 us)
Async XLA Ops:
  0.6 21.2 %copy-start.1 = (s32[512]{0:T(512)S(1)}, s32[512]{0:T(512)}, u32[]{:S(2)}) copy-start(s32[512]{0:T(512)} %param.5) | copy-start | bytes 6148
  21.9 12.6 %copy-start.2 = (s32[128]{0:T(128)S(1)}, s32[128]{0:T(128)}, u32[]{:S(2)}) copy-start(s32[128]{0:T(128)} %param.6) | copy-start | bytes 1540
  30.7 12.6 %collective-permute-start = (bf16[2,512,384]{1,2,0:T(8,128)(2,1)S(1)}, bf16[2,512,384]{1,2,0:T(8,128)(2,1)S(1)}, u32[]{:S(2)}, u32[]{:S(2)}) collective-permute-start(bf16[2,512,384]{1,2,0:T(8,128)(2,1)S(1)} %slice.40), channel_id=1, source_target_pairs={{0,1},{1,2},{2,3},{3,4},{4,5},{5,6},{6,7},{7,8},{8,9},{9,10},{10,1... | collective-permute-start | bytes 2359304 | tf_op jit(solution)/shard_map/ppermute | solution.py:19
  959.8 18.7 %copy-start = (f32[16,64,128]{2,1,0:T(8,128)S(1)}, f32[16,64,128]{2,1,0:T(8,128)}, u32[]{:S(2)}) copy-start(f32[16,64,128]{2,1,0:T(8,128)} %get-tuple-element.13) | copy-start | bytes 1572868

commit v2 on v1

--- a/solution.py
+++ b/solution.py
@@ -143,6 +143,76 @@
 MESH = pl.DeviceIdType.MESH
 
 
+def spectra_kernel(v_ref, h_ref, flag_ref, coeff_ref, table_ref, out_ref, filtered_ref, wide_ref):
+    tile = v_ref.shape[1]
+    frames = v_ref.shape[2] // NCH
+    lanes = 2 * frames
+    flag = jnp.broadcast_to(flag_ref[...], (tile, NCH))
+    rows = [jnp.broadcast_to(coeff_ref[tap : tap + 1, :], (tile, NCH)) for tap in range(TAPS)]
+    for part in range(2):
+
+        def frame_at(index):
+            ref, at = (h_ref, index) if index < TAPS - 1 else (v_ref, index - TAPS + 1)
+            return ref[part, :, at * NCH : (at + 1) * NCH].astype(jnp.float32) * flag
+
+        window = [frame_at(index) for index in range(TAPS - 1)]
+        for frame in range(frames):
+            window = window[-(TAPS - 1) :] + [frame_at(frame + TAPS - 1)]
+            total = rows[0] * window[0]
+            for tap in range(1, TAPS):
+                total = total + rows[tap] * window[tap]
+            filtered_ref[part, frame] = total
+    for first in range(0, tile, 2):
+        stack = []
+        for index in (first, first + 1):
+            re = filtered_ref[0, :, index, :].astype(jnp.bfloat16)
+            im = filtered_ref[1, :, index, :].astype(jnp.bfloat16)
+            stack.append(jnp.concatenate([re, im], axis=1))
+            stack.append(jnp.concatenate([im, -re], axis=1))
+        both = lax.dot_general(
+            table_ref[...],
+            jnp.concatenate(stack, axis=0),
+            (((1,), (1,)), ((), ())),
+            preferred_element_type=jnp.float32,
+        )
+        wide_ref[:, first, :] = both[:, :lanes]
+        wide_ref[:, first + 1, :] = both[:, lanes:]
+    out_ref[...] = wide_ref[...].astype(out_ref.dtype)
+
+
+def spectra_of(voltages, input_flags, channel_order):
+    _, inputs, samples = voltages.shape
+    past = (TAPS - 1) * NCH
+    history = passed_along(voltages[:, :, samples - past :], ("row", "col"), 1)
+    frames = samples // NCH
+    tile = 16
+    tables = dft_tables(channel_order, NCH)[:, 0].reshape(NCH, 2 * NCH)
+    return pl.pallas_call(
+        spectra_kernel,
+        grid=(inputs // tile,),
+        out_shape=jax.ShapeDtypeStruct((NCH, inputs, 2 * frames), jnp.bfloat16),
+        in_specs=[
+            pl.BlockSpec((2, tile, samples), lambda i: (0, i, 0)),
+            pl.BlockSpec((2, tile, past), lambda i: (0, i, 0)),
+            pl.BlockSpec((tile, 1), lambda i: (i, 0)),
+            pl.BlockSpec((TAPS, NCH), lambda i: (0, 0)),
+            pl.BlockSpec((NCH, 2 * NCH), lambda i: (0, 0)),
+        ],
+        out_specs=pl.BlockSpec((NCH, tile, 2 * frames), lambda i: (0, i, 0)),
+        scratch_shapes=[
+            pltpu.VMEM((2, frames, tile, NCH), jnp.float32),
+            pltpu.VMEM((NCH, tile, 2 * frames), jnp.float32),
+        ],
+        name="spectra",
+    )(
+        voltages,
+        history,
+        input_flags.astype(jnp.float32)[:, None],
+        prototype(TAPS, NCH),
+        tables,
+    )
+
+
 def sizes():
     return lax.axis_size("chan"), lax.axis_size("row"), lax.axis_size("col")
 
@@ -158,6 +228,10 @@
     lanes = spec_ref.shape[2]
     beams = weight_ref.shape[2]
 
+    def ahead(step, sign):
+        row = (r + rs + sign * (step % rs)) % rs
+        return row * qs + (q + qs + sign * (step // rs)) % qs
+
     def place(chan, cell):
         return x_ref.at[
             :,
@@ -167,11 +241,11 @@
 
     def spectra(step, outgoing):
         if outgoing:
-            chan, cell = (c + step % cs) % cs, (me + step // cs) % cells
+            chan, cell = (c + step % cs) % cs, ahead(step // cs, 1)
             target = place(c, me)
             slot = here
         else:
-            chan, cell = (c + cs - step % cs) % cs, (me + cells - step // cs) % cells
+            chan, cell = (c + cs - step % cs) % cs, ahead(step // cs, -1)
             target = place(chan, cell)
             slot = chan * cells + cell
         return pltpu.make_async_remote_copy(
@@ -269,6 +343,10 @@
     me = r * qs + q
     own, height, width = vis_ref.shape[1], block_ref.shape[2], block_ref.shape[3]
 
+    def ahead(step, sign):
+        row = (r + rs + sign * (step % rs)) % rs
+        return row * qs + (q + qs + sign * (step // rs)) % qs
+
     def piece(row, col):
         return vis_ref.at[
             :,
@@ -279,10 +357,10 @@
 
     def copies(step, outgoing):
         if outgoing:
-            cell = (me + step) % cells
+            cell = ahead(step, 1)
             slot = me
         else:
-            cell = (me + cells - step) % cells
+            cell = ahead(step, -1)
             slot = cell
         device = (c, cell // qs, cell % qs)
         block = pltpu.make_async_remote_copy(
@@ -421,7 +499,7 @@
 
 def by_channels(voltages, input_flags, channel_order, beam_weights):
     _, rs, qs = sizes()
-    spectrum = channelize(voltages, input_flags, channel_order)
+    spectrum = spectra_of(voltages, input_flags, channel_order)
     frames = spectrum.shape[2] // 2
     x, weights = turn(spectrum, beam_weights)
     visibility, power = products(x, weights, frames)
@@ -436,7 +514,7 @@
 def on_device(voltages, input_flags, channel_order, beam_weights):
     cs, rs, qs = sizes()
     lanes = 2 * (voltages.shape[2] // NCH)
-    if NCH % (cs * rs * qs) == 0 and lanes % 128 == 0:
+    if NCH % (cs * rs * qs) == 0 and lanes % 128 == 0 and voltages.shape[1] % 16 == 0:
         plan = by_channels
     else:
         plan = by_panels

time: 983 us -> 941 us (0.957)
  Pallas kernels: 828 us -> 900 us
  local copies, waits for them, and re-layouts: 72.5 us -> 8.79 us
  matrix products: 30.7 us -> 0 us
  other arithmetic: 38 us -> 23.5 us
    pallas_call x0 -> x1, Pallas kernels: none -> 88.3 us  [spectra_of(): pl.pallas_call(spectra_kernel, grid=(inputs // tile,), out_shape=jax.Shap...]
    dot_general x1 -> x0, matrix products: 30.7 us -> none  [channelize(): jnp.einsum('kqpn,pifn->kiqf', tables.astype(jnp.float32), filtered.astype...]
    convert_element_type x1 -> x0, local copies, waits for them, and re-layouts: 23.3 us -> none  [channelize(): spectrum = jnp.einsum('kqpn,pifn->kiqf', tables.astype(jnp.float32), filt...]
    reshape x1 -> x0, local copies, waits for them, and re-layouts: 22.1 us -> none  [channelize(): spectrum = spectrum.reshape(NCH, local_inputs, 2 * frames)]
    unnamed x8 -> x5, local copies, waits for them, and re-layouts: 22.8 us -> 2.45 us
    pallas_call x1, Pallas kernels: 387 us -> 371 us  [turn(): pl.pallas_call(functools.partial(turn_kernel, cs, rs, qs), out_shape=(jax...]
  transfers between devices with their start and end apart: 1 -> 1, of which waited for: 1 -> 1; matrix products, arithmetic and copies ran while one was open for 0% -> 1% of each run, Pallas kernels for 0% -> 0%
where the time goes in v2:
time: 941 us; the launch traced here: 940 us
  Pallas kernels  900 us (96%)
  other arithmetic  23.5 us (2%)
    pallas_call x1, Pallas kernels, deliver(): pl.pallas_call(functools.partial(deliver_kernel, rs, qs), out_shape=(jax....  378 us
    pallas_call x1, Pallas kernels, turn(): pl.pallas_call(functools.partial(turn_kernel, cs, rs, qs), out_shape=(jax...  371 us
    pallas_call x1, Pallas kernels, spectra_of(): pl.pallas_call(spectra_kernel, grid=(inputs // tile,), out_shape=jax.Shap...  88.3 us
    pallas_call x1, Pallas kernels, products(): pl.pallas_call(functools.partial(products_kernel, depth // 2, min(inputs,...  62.6 us
  transfers between devices with their start and end apart: 1, of which 1 were waited for; matrix products, arithmetic and copies ran while one was open for 1% of the time, Pallas kernels for 0%

profile of v2, /device:TPU:13, one launch (start us, length us, event | category | flops | bytes accessed | tf_op | source)
XLA Modules:
  0.0 939.9 jit_solution(6309187181102188039)
XLA Ops:
  0.6 1.2 slice.4
  1.8 3.7 collective-permute-start
  5.6 0.6 fusion.18.coeff_ref
  6.2 1.0 multiply_convert_fusion.1
  7.2 0.7 convert_element_type.31
  7.9 0.9 copy.13.flag_ref
  8.8 0.6 copy_bitcast_fusion.table_ref
  9.4 0.7 subtract_convert_fusion.swap_ref
  10.1 1.1 select_convert_fusion.pool_ref
  11.3 3.2 collective-permute-done.h_ref
  14.5 0.0 copy-start
  14.5 0.9 copy-done
  15.4 88.3 %spectra.1.spec_ref = bf16[128,512,128]{2,1,0:T(8,128)(2,1)} custom-call(bf16[2,512,8192]{2,1,0:T(8,128)(2,1)} %v_ref.1, bf16[2,512,384]{2,1,0:T(8,128)(2,1)} %copy-done, f32[512,1]{1,0:T(8,128)} %copy.13.flag_ref, f32[4,128]{1,0:T(4,128)} %fusion.18.coeff_ref, bf16[128,256]{1,0:T(8,128)(2,1)} %copy_bitcast_fusion.table_ref), custom_call_target="tpu_custom_call" | custom-call | tf_op jit(solution)/shard_map/spectra/pallas_call | solution.py:190
  103.7 370.6 %turn.1 = (bf16[4,1024,2048]{2,1,0:T(8,128)(2,1)}, bf16[2,4,256,1024]{3,2,1,0:T(8,128)(2,1)}) custom-call(bf16[128,512,128]{2,1,0:T(8,128)(2,1)} %spectra.1.spec_ref, bf16[2,64,64,1024]{3,2,1,0:T(8,128)(2,1)} %weight_ref.1), custom_call_target="tpu_custom_call" | custom-call | tf_op jit(solution)/shard_map/turn/pallas_call | solution.py:316
  474.3 62.6 %products.1 = (bf16[2,4,1024,1024]{3,2,1,0:T(8,128)(2,1)}, f32[4,256,128]{2,1,0:T(8,128)}) custom-call(bf16[4,1024,2048]{2,1,0:T(8,128)(2,1)} %get-tuple-element.8.x_ref, bf16[2,4,256,1024]{3,2,1,0:T(8,128)(2,1)} %get-tuple-element.9.w_ref, bf16[128,128]{1,0:T(8,128)(2,1)} %subtract_convert_fusion.swap_ref, bf16[2048,128]{1,0:T(8,128)(2,1)} %select_convert_fusion.pool_ref), custom_call_target="tpu_custom_call" | custom-call | tf_op jit(solution)/shard_map/products/pallas_call | solution.py:477
  536.9 1.2 copy.14
  538.2 0.5 reshape.200
  538.6 0.8 copy.15
  539.5 1.3 reshape.201.power_ref
  540.7 378.4 %deliver.1 = (bf16[2,64,256,256]{3,2,1,0:T(8,128)(2,1)}, f32[16,64,128]{2,1,0:T(8,128)}) custom-call(bf16[2,4,1024,1024]{3,2,1,0:T(8,128)(2,1)} %get-tuple-element.10.vis_ref, f32[16,64,128]{2,1,0:T(8,128)} %reshape.201.power_ref), custom_call_target="tpu_custom_call" | custom-call | tf_op jit(solution)/shard_map/deliver/pallas_call | solution.py:412
  919.2 0.0 copy-start.1
  919.2 18.7 %convert_element_type.35 = f32[2,64,256,256]{3,2,1,0:T(8,128)} convert(bf16[2,64,256,256]{3,2,1,0:T(8,128)(2,1)} %get-tuple-element.12) | non-fusion elementwise | flops 8388608 | bytes 50331648 | tf_op jit(solution)/shard_map/convert_element_type | solution.py:511
  937.9 0.0 copy-done.1
  937.9 0.5 reshape.202
  938.3 1.6 copy.16
  (2 shorter events, 0.0 us)
Async XLA Ops:
  1.8 12.6 %collective-permute-start = (bf16[2,512,384]{2,1,0:T(8,128)(2,1)S(1)}, bf16[2,512,384]{2,1,0:T(8,128)(2,1)S(1)}, u32[]{:S(2)}, u32[]{:S(2)}) collective-permute-start(bf16[2,512,384]{2,1,0:T(8,128)(2,1)S(1)} %slice.4), channel_id=1, source_target_pairs={{0,1},{1,2},{2,3},{3,4},{4,5},{5,6},{6,7},{7,8},{8,9},{9,10},{10,1... | collective-permute-start | bytes 2359304 | tf_op jit(solution)/shard_map/ppermute | solution.py:19
  14.5 0.9 copy-start
  919.2 18.7 %copy-start.1 = (f32[16,64,128]{2,1,0:T(8,128)S(1)}, f32[16,64,128]{2,1,0:T(8,128)}, u32[]{:S(2)}) copy-start(f32[16,64,128]{2,1,0:T(8,128)} %get-tuple-element.13) | copy-start | bytes 1572868

commit v3 on v0

--- a/solution.py
+++ b/solution.py
@@ -1,8 +1,11 @@
+import functools
 import math
 
 import jax
 import jax.numpy as jnp
 from jax import lax
+from jax.experimental import pallas as pl
+from jax.experimental.pallas import tpu as pltpu
 from jax.sharding import PartitionSpec as P
 
 NCH = 128
@@ -90,7 +93,7 @@
     return power.reshape(power.shape[0], power.shape[1], -1, INTEG).mean(axis=-1)
 
 
-def on_device(voltages, input_flags, channel_order, beam_weights):
+def channelize(voltages, input_flags, channel_order):
     masked = voltages * input_flags.astype(jnp.bfloat16)[None, :, None]
     local_inputs = masked.shape[1]
     frames = masked.shape[2] // NCH
@@ -112,6 +115,12 @@
         precision=lax.Precision.HIGHEST,
     ).astype(jnp.bfloat16)
     spectrum = spectrum.reshape(NCH, local_inputs, 2 * frames)
+    return spectrum
+
+
+def by_panels(voltages, input_flags, channel_order, beam_weights):
+    spectrum = channelize(voltages, input_flags, channel_order)
+    frames = spectrum.shape[2] // 2
     turned = lax.all_to_all(spectrum, "chan", split_axis=0, concat_axis=1, tiled=True)
     row_count = lax.axis_size("row")
     col_count = lax.axis_size("col")
@@ -131,6 +140,434 @@
     return (visibility, beam_power)
 
 
+MESH = pl.DeviceIdType.MESH
+
+
+def spectra_tile(v_ref, h_ref, flag_ref, coeff_ref, table_ref, filtered_ref, wide_ref):
+    tile = v_ref.shape[1]
+    frames = v_ref.shape[2] // NCH
+    lanes = 2 * frames
+    flag = jnp.broadcast_to(flag_ref[...], (tile, NCH))
+    rows = [jnp.broadcast_to(coeff_ref[tap : tap + 1, :], (tile, NCH)) for tap in range(TAPS)]
+    for part in range(2):
+
+        def frame_at(index):
+            ref, at = (h_ref, index) if index < TAPS - 1 else (v_ref, index - TAPS + 1)
+            return ref[part, :, at * NCH : (at + 1) * NCH].astype(jnp.float32) * flag
+
+        window = [frame_at(index) for index in range(TAPS - 1)]
+        for frame in range(frames):
+            window = window[-(TAPS - 1) :] + [frame_at(frame + TAPS - 1)]
+            total = rows[0] * window[0]
+            for tap in range(1, TAPS):
+                total = total + rows[tap] * window[tap]
+            filtered_ref[part, frame] = total
+    for first in range(0, tile, 2):
+        stack = []
+        for index in (first, first + 1):
+            re = filtered_ref[0, :, index, :].astype(jnp.bfloat16)
+            im = filtered_ref[1, :, index, :].astype(jnp.bfloat16)
+            stack.append(jnp.concatenate([re, im], axis=1))
+            stack.append(jnp.concatenate([im, -re], axis=1))
+        both = lax.dot_general(
+            table_ref[...],
+            jnp.concatenate(stack, axis=0),
+            (((1,), (1,)), ((), ())),
+            preferred_element_type=jnp.float32,
+        )
+        wide_ref[:, first, :] = both[:, :lanes]
+        wide_ref[:, first + 1, :] = both[:, lanes:]
+    return wide_ref[...].astype(jnp.bfloat16)
+
+
+def sizes():
+    return lax.axis_size("chan"), lax.axis_size("row"), lax.axis_size("col")
+
+
+def turn_kernel(
+    cs, rs, qs, tile, group,
+    v_ref, h_ref, flag_ref, coeff_ref, table_ref, weight_ref, x_ref, w_ref,
+    filtered_ref, wide_ref, spec_ref, send, recv, wsend, wrecv, local,
+):
+    c, r, q = (lax.axis_index(name) for name in ("chan", "row", "col"))
+    cells = rs * qs
+    devices = cs * cells
+    me = r * qs + q
+    here = c * cells + me
+    own = spec_ref.shape[0] // devices
+    inputs = spec_ref.shape[1]
+    lanes = spec_ref.shape[2]
+    beams = weight_ref.shape[2]
+    turn_step = pl.program_id(0)
+    tiles = inputs // tile
+
+    def ahead(step, sign):
+        row = (r + rs + sign * (step % rs)) % rs
+        return row * qs + (q + qs + sign * (step // rs)) % qs
+
+    def spectra(step, outgoing, first, count):
+        if outgoing:
+            chan, cell = (c + step % cs) % cs, ahead(step // cs, 1)
+            origin, column = c, me
+            slot = here
+        else:
+            chan, cell = (c + cs - step % cs) % cs, ahead(step // cs, -1)
+            origin, column = chan, cell
+            slot = chan * cells + cell
+        return pltpu.make_async_remote_copy(
+            src_ref=spec_ref.at[
+                pl.ds((chan * cells + cell) * own, own),
+                pl.ds(pl.multiple_of(first, tile), count),
+            ],
+            dst_ref=x_ref.at[
+                :,
+                pl.ds(pl.multiple_of(origin * inputs + first, tile), count),
+                pl.ds(pl.multiple_of(column * lanes, lanes), lanes),
+            ],
+            send_sem=send.at[chan * cells + cell],
+            recv_sem=recv.at[slot],
+            device_id=(chan, cell // qs, cell % qs),
+            device_id_type=MESH,
+        )
+
+    def weights(step, outgoing):
+        if outgoing:
+            peer = (q + step) % qs
+            slot = q
+        else:
+            peer = (q + qs - step) % qs
+            slot = peer
+        return pltpu.make_async_remote_copy(
+            src_ref=weight_ref.at[:, pl.ds((r * qs + peer) * own, own)],
+            dst_ref=w_ref.at[:, :, pl.ds(pl.multiple_of(slot * beams, beams), beams)],
+            send_sem=wsend.at[peer],
+            recv_sem=wrecv.at[slot],
+            device_id=(c, r, peer),
+            device_id_type=MESH,
+        )
+
+    keep = pltpu.make_async_copy(
+        weight_ref.at[:, pl.ds(me * own, own)],
+        w_ref.at[:, :, pl.ds(pl.multiple_of(q * beams, beams), beams)],
+        local.at[1],
+    )
+
+    @pl.when(turn_step == 0)
+    def _():
+        def start_weights(step, carry):
+            weights(step, True).start()
+            return carry
+
+        lax.fori_loop(1, qs, start_weights, 0)
+        keep.start()
+
+    @pl.when((turn_step > 0) & (turn_step * tile % group == 0))
+    def _():
+        def start(step, carry):
+            spectra(step, True, turn_step * tile - group, group).start()
+            return carry
+
+        lax.fori_loop(1, devices, start, 0)
+
+    @pl.when(turn_step < tiles)
+    def _():
+        at = pl.ds(pl.multiple_of(turn_step * tile, tile), tile)
+        spec_ref[:, at, :] = spectra_tile(
+            v_ref, h_ref, flag_ref, coeff_ref, table_ref, filtered_ref, wide_ref
+        )
+
+    @pl.when(turn_step == tiles)
+    def _():
+        stay = pltpu.make_async_copy(
+            spec_ref.at[pl.ds(here * own, own)],
+            x_ref.at[
+                :,
+                pl.ds(pl.multiple_of(c * inputs, inputs), inputs),
+                pl.ds(pl.multiple_of(me * lanes, lanes), lanes),
+            ],
+            local.at[0],
+        )
+        stay.start()
+
+        def finish(step, carry):
+            spectra(step, True, 0, inputs).wait_send()
+            spectra(step, False, 0, inputs).wait_recv()
+            return carry
+
+        def finish_weights(step, carry):
+            weights(step, True).wait_send()
+            weights(step, False).wait_recv()
+            return carry
+
+        lax.fori_loop(1, devices, finish, 0)
+        lax.fori_loop(1, qs, finish_weights, 0)
+        stay.wait()
+        keep.wait()
+
+
+def turn(voltages, input_flags, channel_order, beam_weights):
+    cs, rs, qs = sizes()
+    devices = cs * rs * qs
+    own = NCH // devices
+    _, inputs, samples = voltages.shape
+    past = (TAPS - 1) * NCH
+    history = passed_along(voltages[:, :, samples - past :], ("row", "col"), 1)
+    frames = samples // NCH
+    lanes = 2 * frames
+    tile = 16
+    group = 4 * tile if inputs % (4 * tile) == 0 else tile
+    last = inputs // tile - 1
+    tables = dft_tables(channel_order, NCH)[:, 0].reshape(NCH, 2 * NCH)
+    anywhere = pl.BlockSpec(memory_space=pl.ANY)
+    return pl.pallas_call(
+        functools.partial(turn_kernel, cs, rs, qs, tile, group),
+        grid=(inputs // tile + 1,),
+        out_shape=(
+            jax.ShapeDtypeStruct((own, inputs * cs, lanes * rs * qs), jnp.bfloat16),
+            jax.ShapeDtypeStruct(
+                (2, own, beam_weights.shape[2] * qs, beam_weights.shape[3]), beam_weights.dtype
+            ),
+        ),
+        in_specs=[
+            pl.BlockSpec((2, tile, samples), lambda i: (0, jnp.minimum(i, last), 0)),
+            pl.BlockSpec((2, tile, past), lambda i: (0, jnp.minimum(i, last), 0)),
+            pl.BlockSpec((tile, 1), lambda i: (jnp.minimum(i, last), 0)),
+            pl.BlockSpec((TAPS, NCH), lambda i: (0, 0)),
+            pl.BlockSpec((NCH, 2 * NCH), lambda i: (0, 0)),
+            anywhere,
+        ],
+        out_specs=(anywhere,) * 2,
+        scratch_shapes=[
+            pltpu.VMEM((2, frames, tile, NCH), jnp.float32),
+            pltpu.VMEM((NCH, tile, lanes), jnp.float32),
+            pltpu.VMEM((NCH, inputs, lanes), jnp.bfloat16),
+            pltpu.SemaphoreType.DMA((devices,)),
+            pltpu.SemaphoreType.DMA((devices,)),
+            pltpu.SemaphoreType.DMA((qs,)),
+            pltpu.SemaphoreType.DMA((qs,)),
+            pltpu.SemaphoreType.DMA((2,)),
+        ],
+        compiler_params=pltpu.CompilerParams(has_side_effects=True, vmem_limit_bytes=60 << 20),
+        name="turn",
+    )(
+        voltages,
+        history,
+        input_flags.astype(jnp.float32)[:, None],
+        prototype(TAPS, NCH),
+        tables,
+        beam_weights,
+    )
+
+
+def products_kernel(
+    rs, qs, frame_count, tile,
+    x_ref, w_ref, swap_ref, pool_ref, block_ref, part_ref,
+    y_ref, vis_ref, power_ref, send, recv, psend, precv, local,
+):
+    c, r, q = (lax.axis_index(name) for name in ("chan", "row", "col"))
+    cells = rs * qs
+    me = r * qs + q
+    own, inputs = vis_ref.shape[0], vis_ref.shape[2]
+    depth = x_ref.shape[2]
+    height, width = block_ref.shape[2], block_ref.shape[3]
+    part_height, part_width = part_ref.shape[1], part_ref.shape[2]
+    channel = pl.program_id(0)
+
+    def ahead(step, sign):
+        row = (r + rs + sign * (step % rs)) % rs
+        return row * qs + (q + qs + sign * (step // rs)) % qs
+
+    def vis_at(first, count, row, col):
+        return vis_ref.at[
+            pl.ds(first, count),
+            :,
+            pl.ds(pl.multiple_of(row * height, height), height),
+            pl.ds(pl.multiple_of(col * width, width), width),
+        ]
+
+    def power_at(row, col):
+        return power_ref.at[
+            pl.ds(pl.multiple_of(col * part_height, part_height), part_height),
+            pl.ds(pl.multiple_of(row * part_width, part_width), part_width),
+        ]
+
+    def ends(step, outgoing):
+        if outgoing:
+            cell = ahead(step, 1)
+            return cell, me
+        cell = ahead(step, -1)
+        return cell, cell
+
+    def block(step, outgoing, first, count):
+        cell, slot = ends(step, outgoing)
+        return pltpu.make_async_remote_copy(
+            src_ref=vis_at(first, count, cell // qs, cell % qs),
+            dst_ref=block_ref.at[pl.ds(slot * own + first, count)],
+            send_sem=send.at[cell],
+            recv_sem=recv.at[slot],
+            device_id=(c, cell // qs, cell % qs),
+            device_id_type=MESH,
+        )
+
+    def part(step, outgoing):
+        cell, slot = ends(step, outgoing)
+        return pltpu.make_async_remote_copy(
+            src_ref=power_at(cell // qs, cell % qs),
+            dst_ref=part_ref.at[slot],
+            send_sem=psend.at[cell],
+            recv_sem=precv.at[slot],
+            device_id=(c, cell // qs, cell % qs),
+            device_id_type=MESH,
+        )
+
+    @pl.when(channel == 0)
+    def _():
+        power_ref[...] = jnp.zeros_like(power_ref)
+
+    @pl.when(channel > 0)
+    def _():
+        def start(step, carry):
+            block(step, True, channel - 1, 1).start()
+            return carry
+
+        lax.fori_loop(1, cells, start, 0)
+
+    @pl.when(channel < own)
+    def _():
+        lanes = swap_ref.shape[0]
+        across = (((1,), (1,)), ((), ()))
+
+        def rows(step, carry):
+            at = pl.ds(pl.multiple_of(step * tile, tile), tile)
+            for start in range(0, depth, lanes):
+                y_ref[at, start : start + lanes] = jnp.dot(
+                    x_ref[0, at, start : start + lanes],
+                    swap_ref[...],
+                    preferred_element_type=jnp.float32,
+                ).astype(jnp.bfloat16)
+            re = lax.dot_general(
+                x_ref[0, at, :], x_ref[0], across, preferred_element_type=jnp.float32
+            )
+            vis_ref[channel, 0, at, :] = (re / frame_count).astype(vis_ref.dtype)
+            im = lax.dot_general(y_ref[at, :], x_ref[0], across, preferred_element_type=jnp.float32)
+            vis_ref[channel, 1, at, :] = (im / frame_count).astype(vis_ref.dtype)
+            return carry
+
+        lax.fori_loop(0, inputs // tile, rows, 0)
+        span = 4 * lanes if depth % (4 * lanes) == 0 else lanes
+
+        def columns(step, carry):
+            at = pl.ds(pl.multiple_of(step * span, span), span)
+            beam = jnp.dot(w_ref[0, 0], x_ref[0, :, at], preferred_element_type=jnp.float32)
+            beam = beam - jnp.dot(w_ref[1, 0], y_ref[:, at], preferred_element_type=jnp.float32)
+            square = beam * beam
+            high = square.astype(jnp.bfloat16)
+            low = (square - high.astype(jnp.float32)).astype(jnp.bfloat16)
+            pool = pool_ref[at, :]
+            return (
+                carry
+                + jnp.dot(high, pool, preferred_element_type=jnp.float32)
+                + jnp.dot(low, pool, preferred_element_type=jnp.float32)
+            )
+
+        found = lax.fori_loop(0, depth // span, columns, jnp.zeros(power_ref.shape, jnp.float32))
+        lane = lax.broadcasted_iota(jnp.int32, power_ref.shape, 1) % part_width
+        power_ref[...] = jnp.where(lane // (part_width // own) == channel, found, power_ref[...])
+
+    @pl.when(channel == own)
+    def _():
+        stay = pltpu.make_async_copy(
+            vis_at(0, own, r, q), block_ref.at[pl.ds(me * own, own)], local.at[0]
+        )
+        keep = pltpu.make_async_copy(power_at(r, q), part_ref.at[me], local.at[1])
+
+        def start(step, carry):
+            part(step, True).start()
+            return carry
+
+        lax.fori_loop(1, cells, start, 0)
+        stay.start()
+        keep.start()
+
+        def finish(step, carry):
+            block(step, True, 0, own).wait_send()
+            block(step, False, 0, own).wait_recv()
+            part(step, True).wait_send()
+            part(step, False).wait_recv()
+            return carry
+
+        lax.fori_loop(1, cells, finish, 0)
+        stay.wait()
+        keep.wait()
+
+
+def products(x, weights, frames):
+    _, rs, qs = sizes()
+    cells = rs * qs
+    own, inputs, depth = x.shape
+    beams = weights.shape[2]
+    bins = depth // (2 * INTEG)
+    lanes = 2 * frames
+    last = own - 1
+    source = jnp.arange(lanes)[:, None]
+    goal = jnp.arange(lanes)[None, :]
+    swap = jnp.where(source == goal + frames, 1.0, 0.0) - jnp.where(source + frames == goal, 1.0, 0.0)
+    at = jnp.arange(depth)
+    frame = at // lanes * frames + at % frames
+    part = bins // rs
+    column = jnp.arange(rs * own * part)
+    bin_of = column // (own * part) * part + column % part
+    pool = jnp.where(frame[:, None] // INTEG == bin_of[None, :], 1.0 / INTEG, 0.0)
+    anywhere = pl.BlockSpec(memory_space=pl.ANY)
+    return pl.pallas_call(
+        functools.partial(products_kernel, rs, qs, depth // 2, min(inputs, 256)),
+        grid=(own + 1,),
+        out_shape=(
+            jax.ShapeDtypeStruct((cells * own, 2, inputs // rs, inputs // qs), jnp.bfloat16),
+            jax.ShapeDtypeStruct((cells, beams // qs, own * part), jnp.float32),
+        ),
+        in_specs=[
+            pl.BlockSpec((1, inputs, depth), lambda j: (jnp.minimum(j, last), 0, 0)),
+            pl.BlockSpec((2, 1, beams, inputs), lambda j: (0, jnp.minimum(j, last), 0, 0)),
+            pl.BlockSpec((lanes, lanes), lambda j: (0, 0)),
+            pl.BlockSpec((depth, rs * own * part), lambda j: (0, 0)),
+        ],
+        out_specs=(anywhere,) * 2,
+        scratch_shapes=[
+            pltpu.VMEM((inputs, depth), jnp.bfloat16),
+            pltpu.VMEM((own, 2, inputs, inputs), jnp.bfloat16),
+            pltpu.VMEM((beams, rs * own * part), jnp.float32),
+        ]
+        + [pltpu.SemaphoreType.DMA((cells,))] * 4
+        + [pltpu.SemaphoreType.DMA((2,))],
+        compiler_params=pltpu.CompilerParams(has_side_effects=True, vmem_limit_bytes=60 << 20),
+        name="products",
+    )(x, weights, swap.astype(jnp.bfloat16), pool.astype(jnp.bfloat16))
+
+
+def by_channels(voltages, input_flags, channel_order, beam_weights):
+    x, weights = turn(voltages, input_flags, channel_order, beam_weights)
+    block, part = products(x, weights, voltages.shape[2] // NCH)
+    own = x.shape[0]
+    cells, beams, _ = part.shape
+    split = part.reshape(cells, beams, own, -1)
+    beam_power = jnp.transpose(split, (0, 2, 1, 3)).reshape(cells * own, beams, -1)
+    visibility = jnp.transpose(block.astype(jnp.float32), (1, 0, 2, 3))
+    return (visibility, beam_power)
+
+
+def on_device(voltages, input_flags, channel_order, beam_weights):
+    cs, rs, qs = sizes()
+    lanes = 2 * (voltages.shape[2] // NCH)
+    devices = cs * rs * qs
+    whole = NCH % devices == 0 and lanes % 128 == 0 and voltages.shape[1] % 16 == 0
+    if whole and NCH // devices * (lanes // 2 * qs // INTEG) % 128 == 0:
+        plan = by_channels
+    else:
+        plan = by_panels
+    return plan(voltages, input_flags, channel_order, beam_weights)
+
+
 def solution(mesh):
     placed = (P(None, "chan", ("row", "col")), P("chan"), P(), P(None, "chan", "col", None))
     return jax.shard_map(

time: 2990 us -> 821 us (0.27)
  blocking collectives: 1260 us -> 0 us
  Pallas kernels: 0 us -> 779 us
  matrix products: 771 us -> 0 us
  waiting for transfers between devices: 494 us -> 2.79 us
  local copies, waits for them, and re-layouts: 295 us -> 17.5 us
  other arithmetic: 124 us -> 14.7 us
    all_to_all x3 -> x0, blocking collectives: 1260 us -> none  [the longest x1 814 us: on_device(): lax.all_to_all(turned, 'row', split_axis=1, concat_axis=2, tiled=True)]
    pallas_call x0 -> x2, Pallas kernels: none -> 779 us  [the longest x1 396 us: products(): pl.pallas_call(functools.partial(products_kernel, rs, qs, depth // 2, min...]
    dot_general x513 -> x0, matrix products: 771 us -> none  [the longest x64 98.7 us: correlate_one(): lax.dot_general(left_re, right_im, dims, preferred_element_type=jnp.float32)]
    all_gather x3 -> x0, waiting for transfers between devices: 479 us -> none  [the longest x1 341 us: on_device(): row_all = lax.all_gather(row_turned, 'col', axis=2, tiled=True)]
    all_to_all x7 -> x0, local copies, waits for them, and re-layouts: 106 us -> none  [the longest x2 53.7 us: on_device(): lax.all_to_all(spectrum, 'chan', split_axis=0, concat_axis=1, tiled=True)]
    transpose x2 -> x0, local copies, waits for them, and re-layouts: 99 us -> none  [the longest x1 54.9 us: to_frames(): order = jnp.transpose(split, (0, 4, 1, 2, 3, 5))]
    dynamic_update_slice x128 -> x0, other arithmetic: 95.9 us -> none  [the longest x64 53.5 us: correlate(): lax.map(lambda items: correlate_one(items[0], items[1], frame_count), (le...]
  transfers between devices with their start and end apart: 5 -> 1, of which waited for: 4 -> 1; matrix products, arithmetic and copies ran while one was open for 23% -> 1% of each run, Pallas kernels for 0% -> 0%
where the time goes in v3:
time: 821 us; the launch traced here: 819 us
  Pallas kernels  779 us (95%)
  local copies, waits for them, and re-layouts  17.5 us (2%)
  other arithmetic  14.7 us (2%)
    pallas_call x1, Pallas kernels, products(): pl.pallas_call(functools.partial(products_kernel, rs, qs, depth // 2, min...  396 us
    pallas_call x1, Pallas kernels, turn(): pl.pallas_call(functools.partial(turn_kernel, cs, rs, qs, tile, group), g...  383 us
  transfers between devices with their start and end apart: 1, of which 1 were waited for; matrix products, arithmetic and copies ran while one was open for 1% of the time, Pallas kernels for 0%

profile of v3, /device:TPU:13, one launch (start us, length us, event | category | flops | bytes accessed | tf_op | source)
XLA Modules:
  0.0 818.6 jit_solution(7667089104605570436)
XLA Ops:
  0.6 1.2 slice.16
  1.8 3.7 collective-permute-start
  5.6 0.7 fusion.22.coeff_ref
  6.2 0.7 convert_element_type.29
  6.9 0.9 copy.30.flag_ref
  7.8 1.0 multiply_convert_fusion.1
  8.8 0.6 copy_bitcast_fusion.table_ref
  9.4 0.7 subtract_convert_fusion.swap_ref
  10.1 1.6 select_convert_fusion.pool_ref
  11.7 2.8 collective-permute-done.h_ref
  14.5 0.0 copy-start.1
  14.5 0.9 copy-done.1
  15.4 382.9 %turn.1 = (bf16[4,1024,2048]{2,1,0:T(8,128)(2,1)}, bf16[2,4,256,1024]{3,2,1,0:T(8,128)(2,1)}) custom-call(bf16[2,512,8192]{2,1,0:T(8,128)(2,1)} %v_ref.1, bf16[2,512,384]{2,1,0:T(8,128)(2,1)} %copy-done.1, f32[512,1]{1,0:T(8,128)} %copy.30.flag_ref, f32[4,128]{1,0:T(4,128)} %fusion.22.coeff_ref, bf16[128,256]{1,0:T(8,128)(2,1)} %copy_bitcast_fusion.table_ref, ...), custom_call_target="tpu_custom_call" | custom-call | tf_op jit(solution)/shard_map/turn/pallas_call | solution.py:322
  398.2 396.3 %products.1 = (bf16[64,2,256,256]{3,2,1,0:T(8,128)(2,1)}, f32[16,64,128]{2,1,0:T(8,128)}) custom-call(bf16[4,1024,2048]{2,1,0:T(8,128)(2,1)} %get-tuple-element.6.x_ref, bf16[2,4,256,1024]{3,2,1,0:T(8,128)(2,1)} %get-tuple-element.7.w_ref, bf16[128,128]{1,0:T(8,128)(2,1)} %subtract_convert_fusion.swap_ref, bf16[2048,512]{1,0:T(8,128)(2,1)} %select_convert_fusion.pool_ref), custom_call_target="tpu_custom_call" | custom-call | tf_op jit(solution)/shard_map/products/pallas_call | solution.py:522
  794.5 9.3 %convert_bitcast_fusion = f32[2,64,256,256]{3,2,0,1:T(8,128)S(1)} fusion(bf16[64,2,256,256]{3,2,1,0:T(8,128)(2,1)} %get-tuple-element.8), kind=kLoop, calls=%fused_computation | loop fusion | flops 8388608 | bytes 50331648 | tf_op jit(solution)/shard_map/transpose | solution.py:555
  803.8 0.0 copy-start
  803.8 12.5 %copy.32 = f32[2,64,256,256]{3,2,1,0:T(8,128)} copy(f32[2,64,256,256]{3,2,0,1:T(8,128)S(1)} %convert_bitcast_fusion) | data formatting | bytes 67108864
  816.3 0.0 copy-done
  816.3 0.5 fusion.29
  816.8 0.2 pad_maximum_fusion
  817.0 1.6 copy.33
  (3 shorter events, 0.0 us)
Async XLA Ops:
  1.8 12.6 %collective-permute-start = (bf16[2,512,384]{2,1,0:T(8,128)(2,1)S(1)}, bf16[2,512,384]{2,1,0:T(8,128)(2,1)S(1)}, u32[]{:S(2)}, u32[]{:S(2)}) collective-permute-start(bf16[2,512,384]{2,1,0:T(8,128)(2,1)S(1)} %slice.16), channel_id=1, source_target_pairs={{0,1},{1,2},{2,3},{3,4},{4,5},{5,6},{6,7},{7,8},{8,9},{9,10},{10,1... | collective-permute-start | bytes 2359304 | tf_op jit(solution)/shard_map/ppermute | solution.py:19
  14.5 0.9 copy-start.1
  803.8 12.5 %copy-start = (f32[16,64,128]{2,1,0:T(8,128)S(1)}, f32[16,64,128]{2,1,0:T(8,128)}, u32[]{:S(2)}) copy-start(f32[16,64,128]{2,1,0:T(8,128)} %get-tuple-element.9) | copy-start | bytes 1572868

commit v4 on v3

--- a/solution.py
+++ b/solution.py
@@ -315,7 +315,7 @@
     frames = samples // NCH
     lanes = 2 * frames
     tile = 16
-    group = 4 * tile if inputs % (4 * tile) == 0 else tile
+    group = 2 * tile if inputs % (2 * tile) == 0 else tile
     last = inputs // tile - 1
     tables = dft_tables(channel_order, NCH)[:, 0].reshape(NCH, 2 * NCH)
     anywhere = pl.BlockSpec(memory_space=pl.ANY)
@@ -367,7 +367,7 @@
     c, r, q = (lax.axis_index(name) for name in ("chan", "row", "col"))
     cells = rs * qs
     me = r * qs + q
-    own, inputs = vis_ref.shape[0], vis_ref.shape[2]
+    own, inputs = vis_ref.shape[1], vis_ref.shape[2]
     depth = x_ref.shape[2]
     height, width = block_ref.shape[2], block_ref.shape[3]
     part_height, part_width = part_ref.shape[1], part_ref.shape[2]
@@ -379,8 +379,8 @@
 
     def vis_at(first, count, row, col):
         return vis_ref.at[
+            :,
             pl.ds(first, count),
-            :,
             pl.ds(pl.multiple_of(row * height, height), height),
             pl.ds(pl.multiple_of(col * width, width), width),
         ]
@@ -402,7 +402,7 @@
         cell, slot = ends(step, outgoing)
         return pltpu.make_async_remote_copy(
             src_ref=vis_at(first, count, cell // qs, cell % qs),
-            dst_ref=block_ref.at[pl.ds(slot * own + first, count)],
+            dst_ref=block_ref.at[:, pl.ds(slot * own + first, count)],
             send_sem=send.at[cell],
             recv_sem=recv.at[slot],
             device_id=(c, cell // qs, cell % qs),
@@ -448,9 +448,9 @@
             re = lax.dot_general(
                 x_ref[0, at, :], x_ref[0], across, preferred_element_type=jnp.float32
             )
-            vis_ref[channel, 0, at, :] = (re / frame_count).astype(vis_ref.dtype)
+            vis_ref[0, channel, at, :] = (re / frame_count).astype(vis_ref.dtype)
             im = lax.dot_general(y_ref[at, :], x_ref[0], across, preferred_element_type=jnp.float32)
-            vis_ref[channel, 1, at, :] = (im / frame_count).astype(vis_ref.dtype)
+            vis_ref[1, channel, at, :] = (im / frame_count).astype(vis_ref.dtype)
             return carry
 
         lax.fori_loop(0, inputs // tile, rows, 0)
@@ -477,7 +477,7 @@
     @pl.when(channel == own)
     def _():
         stay = pltpu.make_async_copy(
-            vis_at(0, own, r, q), block_ref.at[pl.ds(me * own, own)], local.at[0]
+            vis_at(0, own, r, q), block_ref.at[:, pl.ds(me * own, own)], local.at[0]
         )
         keep = pltpu.make_async_copy(power_at(r, q), part_ref.at[me], local.at[1])
 
@@ -523,7 +523,7 @@
         functools.partial(products_kernel, rs, qs, depth // 2, min(inputs, 256)),
         grid=(own + 1,),
         out_shape=(
-            jax.ShapeDtypeStruct((cells * own, 2, inputs // rs, inputs // qs), jnp.bfloat16),
+            jax.ShapeDtypeStruct((2, cells * own, inputs // rs, inputs // qs), jnp.bfloat16),
             jax.ShapeDtypeStruct((cells, beams // qs, own * part), jnp.float32),
         ),
         in_specs=[
@@ -535,7 +535,7 @@
         out_specs=(anywhere,) * 2,
         scratch_shapes=[
             pltpu.VMEM((inputs, depth), jnp.bfloat16),
-            pltpu.VMEM((own, 2, inputs, inputs), jnp.bfloat16),
+            pltpu.VMEM((2, own, inputs, inputs), jnp.bfloat16),
             pltpu.VMEM((beams, rs * own * part), jnp.float32),
         ]
         + [pltpu.SemaphoreType.DMA((cells,))] * 4
@@ -552,8 +552,7 @@
     cells, beams, _ = part.shape
     split = part.reshape(cells, beams, own, -1)
     beam_power = jnp.transpose(split, (0, 2, 1, 3)).reshape(cells * own, beams, -1)
-    visibility = jnp.transpose(block.astype(jnp.float32), (1, 0, 2, 3))
-    return (visibility, beam_power)
+    return (block.astype(jnp.float32), beam_power)
 
 
 def on_device(voltages, input_flags, channel_order, beam_weights):

time: 821 us -> 812 us (0.989)
  local copies, waits for them, and re-layouts: 17.5 us -> 5.01 us
  other arithmetic: 14.7 us -> 24.1 us
    convert_element_type x0 -> x1, other arithmetic: none -> 18.7 us  [by_channels(): return (block.astype(jnp.float32), beam_power)]
    unnamed x6 -> x5, local copies, waits for them, and re-layouts: 15 us -> 2.45 us
    transpose x1 -> x0, other arithmetic: 9.28 us -> none  [by_channels(): visibility = jnp.transpose(block.astype(jnp.float32), (1, 0, 2, 3))]
where the time goes in v4:
time: 812 us; the launch traced here: 809 us
  Pallas kernels  773 us (95%)
  other arithmetic  24.1 us (3%)
    pallas_call x1, Pallas kernels, products(): pl.pallas_call(functools.partial(products_kernel, rs, qs, depth // 2, min...  396 us
    pallas_call x1, Pallas kernels, turn(): pl.pallas_call(functools.partial(turn_kernel, cs, rs, qs, tile, group), g...  377 us
    convert_element_type x1, other arithmetic, by_channels(): return (block.astype(jnp.float32), beam_power)  18.7 us
  transfers between devices with their start and end apart: 1, of which 1 were waited for; matrix products, arithmetic and copies ran while one was open for 1% of the time, Pallas kernels for 0%

profile of v4, /device:TPU:13, one launch (start us, length us, event | category | flops | bytes accessed | tf_op | source)
XLA Modules:
  0.0 809.4 jit_solution(5799313876765181953)
XLA Ops:
  0.6 1.2 slice.16
  1.8 3.7 collective-permute-start
  5.6 0.7 fusion.22.coeff_ref
  6.2 0.7 convert_element_type.31
  6.9 0.9 copy.25.flag_ref
  7.8 1.0 multiply_convert_fusion.1
  8.8 0.6 copy_bitcast_fusion.table_ref
  9.4 0.7 subtract_convert_fusion.swap_ref
  10.1 1.6 select_convert_fusion.pool_ref
  11.7 2.8 collective-permute-done.h_ref
  14.5 0.0 copy-start.1
  14.5 0.9 copy-done.1
  15.4 376.9 %turn.1 = (bf16[4,1024,2048]{2,1,0:T(8,128)(2,1)}, bf16[2,4,256,1024]{3,2,1,0:T(8,128)(2,1)}) custom-call(bf16[2,512,8192]{2,1,0:T(8,128)(2,1)} %v_ref.1, bf16[2,512,384]{2,1,0:T(8,128)(2,1)} %copy-done.1, f32[512,1]{1,0:T(8,128)} %copy.25.flag_ref, f32[4,128]{1,0:T(4,128)} %fusion.22.coeff_ref, bf16[128,256]{1,0:T(8,128)(2,1)} %copy_bitcast_fusion.table_ref, ...), custom_call_target="tpu_custom_call" | custom-call | tf_op jit(solution)/shard_map/turn/pallas_call | solution.py:322
  392.3 396.2 %products.1 = (bf16[2,64,256,256]{3,2,1,0:T(8,128)(2,1)}, f32[16,64,128]{2,1,0:T(8,128)}) custom-call(bf16[4,1024,2048]{2,1,0:T(8,128)(2,1)} %get-tuple-element.6.x_ref, bf16[2,4,256,1024]{3,2,1,0:T(8,128)(2,1)} %get-tuple-element.7.w_ref, bf16[128,128]{1,0:T(8,128)(2,1)} %subtract_convert_fusion.swap_ref, bf16[2048,512]{1,0:T(8,128)(2,1)} %select_convert_fusion.pool_ref), custom_call_target="tpu_custom_call" | custom-call | tf_op jit(solution)/shard_map/products/pallas_call | solution.py:522
  788.5 0.0 copy-start
  788.5 18.7 %convert_element_type.35 = f32[2,64,256,256]{3,2,1,0:T(8,128)} convert(bf16[2,64,256,256]{3,2,1,0:T(8,128)(2,1)} %get-tuple-element.8) | non-fusion elementwise | flops 8388608 | bytes 50331648 | tf_op jit(solution)/shard_map/convert_element_type | solution.py:555
  807.2 0.0 copy-done
  807.2 0.5 fusion.29
  807.6 0.2 pad_maximum_fusion
  807.8 1.6 copy.27
  (3 shorter events, 0.0 us)
Async XLA Ops:
  1.8 12.6 %collective-permute-start = (bf16[2,512,384]{2,1,0:T(8,128)(2,1)S(1)}, bf16[2,512,384]{2,1,0:T(8,128)(2,1)S(1)}, u32[]{:S(2)}, u32[]{:S(2)}) collective-permute-start(bf16[2,512,384]{2,1,0:T(8,128)(2,1)S(1)} %slice.16), channel_id=1, source_target_pairs={{0,1},{1,2},{2,3},{3,4},{4,5},{5,6},{6,7},{7,8},{8,9},{9,10},{10,1... | collective-permute-start | bytes 2359304 | tf_op jit(solution)/shard_map/ppermute | solution.py:19
  14.5 0.9 copy-start.1
  788.5 18.7 %copy-start = (f32[16,64,128]{2,1,0:T(8,128)S(1)}, f32[16,64,128]{2,1,0:T(8,128)}, u32[]{:S(2)}) copy-start(f32[16,64,128]{2,1,0:T(8,128)} %get-tuple-element.9) | copy-start | bytes 1572868
